TPU v7x, 32 devices: a whole 2x2x4 slice. The times are simulated.
32 devices in a mesh: row: 4 (over z), col: 8 (over y, x, core).
Axes of the slice: x: 2, y: 2, z: 4, core: 2. Of those that a mesh axis runs over, the one named last changes fastest.
Arguments:
- q_halves: float32 [2, 5120, 5120], P(None, 'row', 'col'), may hold values from -6 to 6
- pole_values: float32 [10240], replicated, may hold values from -10240 to 10240, as said below
- weights: float32 [10240], replicated, may hold values from -6 to 6
- secular_roots: float32 [10240], replicated, may hold values from -10240 to 20480, as said below
- column_order: int32 [10240], replicated, may hold values from 0 to 10239, each once
- deflated: int32 [10240], replicated, may hold values 0 or 1
- reflectors: float32 [2, 2, 5120, 256], P(None, None, 'row'), may hold values from -0.0625 to 0.0625
- triangles: float32 [2, 256, 256], replicated, may hold values from -1.5 to 1.5
Outputs:
- eigvecs: float32 [2, 5120, 10240], P(None, 'row', 'col')
Inputs may be any that keep to these rules, and one draw needn't show every extreme that they name: `pole_values`: all distinct; sorted, neighbouring poles differ by 0.5 to 1.5. The order of the entries is not sorted. secular_roots[j] lies above pole_values[j], at a quarter to three quarters of the distance to the next larger pole (for the largest pole, of a distance of 0.5 to 1.5), so every pole differs from every root by an eighth or more.
All inputs are finite; a program needn't handle non-finite values.
Results may differ from a plain program's by a relative error of at most 0.00015.
Values sent between devices are 32-bit elements; how exact they have to be, the bound alone decides.
No kernel may reach another device: no remote copies, remote signals or barrier semaphores. Data moves between devices by JAX's collectives and lax.ppermute only.
A program may use at most 192 MiB of HBM per device.

v0:
```python
import functools

import jax
import jax.numpy as jnp
from jax import lax
from jax.experimental import pallas as pl
from jax.experimental.pallas import tpu as pltpu
from jax.sharding import PartitionSpec as P


EPSILON = 1e-06
FAR = 3e38


def split2(x):
    high = x.astype(jnp.bfloat16)
    return high, (x - high.astype(jnp.float32)).astype(jnp.bfloat16)


def dot3(a_high, a_low, b_high, b_low):
    dot = functools.partial(jnp.dot, preferred_element_type=jnp.float32)
    return dot(a_high, b_high) + (dot(a_high, b_low) + dot(a_low, b_high))


def cauchy_kernel(pole_ref, zed_ref, root_ref, key_ref, high_ref, low_ref, total_ref):
    step = pl.program_id(0)
    rows = pole_ref.shape[0]

    @pl.when(step == 0)
    def _():
        total_ref[...] = jnp.zeros_like(total_ref)

    ratio = zed_ref[...] / (pole_ref[...] - root_ref[...])
    total_ref[...] += jnp.sum(ratio * ratio, axis=0, keepdims=True)
    row_ids = step * rows + lax.broadcasted_iota(jnp.int32, ratio.shape, 0)
    value = jnp.where(row_ids == key_ref[...], 1.0, ratio)
    high_ref[...], low_ref[...] = split2(value)


def make_cauchy(poles, zeds, roots, keys):
    count, width = poles.shape[0], roots.shape[0]
    rows = 256
    vec = pl.BlockSpec((rows, 1), lambda i: (i, 0))
    line = pl.BlockSpec((1, width), lambda i: (0, 0))
    tile = pl.BlockSpec((rows, width), lambda i: (i, 0))
    part = jax.ShapeDtypeStruct((count, width), jnp.bfloat16)
    return pl.pallas_call(
        cauchy_kernel,
        grid=(count // rows,),
        in_specs=[vec, vec, line, line],
        out_specs=[tile, tile, line],
        out_shape=[part, part, jax.ShapeDtypeStruct((1, width), jnp.float32)],
        name="cauchy",
    )(poles[:, None], zeds[:, None], roots[None, :], keys[None, :])


def early_kernel(r_ref, ch_ref, cl_ref, o_ref, high, low):
    @pl.when(pl.program_id(0) == 0)
    def _():
        for h in range(2):
            half = r_ref.shape[2]
            high[:, h * half : (h + 1) * half], low[:, h * half : (h + 1) * half] = split2(r_ref[h])

    o_ref[...] = dot3(high[...], low[...], ch_ref[...], cl_ref[...])


def early_projection(r_all, c_high, c_low):
    _, rows, _ = r_all.shape
    count, width = c_high.shape
    tile = 128
    col = pl.BlockSpec((count, tile), lambda j: (0, j))
    return pl.pallas_call(
        early_kernel,
        grid=(width // tile,),
        in_specs=[pl.BlockSpec(r_all.shape, lambda j: (0, 0, 0)), col, col],
        out_specs=pl.BlockSpec((rows, tile), lambda j: (0, j)),
        out_shape=jax.ShapeDtypeStruct((rows, width), jnp.float32),
        scratch_shapes=[pltpu.VMEM((rows, count), jnp.bfloat16)] * 2,
        name="early",
    )(r_all, c_high, c_low)


def rows_kernel(counts, last, info_ref, *refs):
    refs = list(refs)
    pairs, parts, rows = counts
    sources = [[[refs.pop(0) for _ in range(parts)] for _ in range(2)] for _ in range(pairs)]
    high_ref, low_ref = refs.pop(0), refs.pop(0)
    if last:
        first_y, second_y, s_ref, scale_ref, acc_ref = (refs.pop(0) for _ in range(5))
    refs = refs[1:] if last == 2 else refs
    out_ref, staged, q_high, q_low, sems = refs[:5]
    depth = staged.shape[3]
    step, col = pl.program_id(0), pl.program_id(1)
    half, block, odd = info_ref[0], info_ref[1], info_ref[2]

    def copies(i):
        for core in range(2):
            slot = odd if core == 0 else 1 - odd
            for part in range(parts):
                ref = sources[i][core][part]
                if len(ref.shape) == 3:
                    ref = ref.at[half, pl.ds((block * parts + part) * rows, rows)]
                yield pltpu.make_async_copy(
                    ref, staged.at[slot, part], sems.at[core, part]
                )

    @pl.when(jnp.logical_and(step == 0, col == 0))
    def _():
        for copy in copies(0):
            copy.start()

    for i in range(pairs):

        @pl.when(jnp.logical_and(step == i, col == 0))
        def _():
            for copy in copies(i):
                copy.wait()
            for core in range(2):
                for part in range(parts):
                    at = (slice(part * rows, (part + 1) * rows), slice(core * depth, (core + 1) * depth))
                    q_high[at], q_low[at] = split2(staged[core, part])
            if i + 1 < pairs:
                for copy in copies(i + 1):
                    copy.start()

    product = dot3(q_high[...], q_low[...], high_ref[...], low_ref[...])

    def emit(mixed):
        if not last:
            out_ref[...] = mixed
            return
        size = first_y.shape[3]
        y_high, y_low = refs[5:7]

        @pl.when(col == 0)
        def _():
            y_high[:, :size], y_low[:, :size] = split2(first_y[0, 0])
            y_high[:, size:], y_low[:, size:] = split2(second_y[0, 0])

        update = dot3(y_high[...], y_low[...], *split2(s_ref[...]))
        out_ref[0] = (acc_ref[...] + mixed - update) * scale_ref[...]

    if pairs == 1:
        emit(product)
    else:
        total = refs[-1]

        @pl.when(step == 0)
        def _():
            total[col] = product

        if pairs > 2:

            @pl.when(jnp.logical_and(step > 0, step < pairs - 1))
            def _():
                total[col] += product

        @pl.when(step == pairs - 1)
        def _():
            emit(total[col] + product)


def rows_call(half, block, masks, pieces, c_high, c_low, finish=None):
    me = lax.axis_index("col")
    chips = lax.axis_size("col") // 2
    pairs, parts = len(masks), len(pieces[0][0])
    rows, depth = pieces[-1][0][0].shape[-2:]
    width = c_high.shape[1]
    tile = 256 if width % 256 == 0 else 128
    head = [jnp.int32(half), jnp.int32(block), me & 1]
    info = jnp.stack(head + [half * chips + ((me ^ m) >> 1) for m in masks]).astype(jnp.int32)

    operands = [array for pair in pieces for piece in pair for array in piece]
    in_specs = [pl.BlockSpec(memory_space=pl.ANY)] * len(operands)
    cauchy = pl.BlockSpec((2 * depth, tile), lambda i, j, info: (info[3 + i], j))
    in_specs += [cauchy, cauchy]
    operands += [c_high, c_low]
    count = parts * rows
    scratch = [pltpu.VMEM((2, parts, rows, depth), jnp.float32)]
    scratch += [pltpu.VMEM((count, 2 * depth), jnp.bfloat16)] * 2
    scratch += [pltpu.SemaphoreType.DMA((2, parts))]
    aliases, last = {}, 0
    if finish is None:
        out_shape = (count, width)
        out_spec = pl.BlockSpec((count, tile), lambda i, j, info: (0, jnp.where(i == pairs - 1, j, 0)))
    else:
        reflectors, s, scale, held, out = finish
        last = 1 if out is None else 2
        size = reflectors.shape[3]
        in_specs += [
            pl.BlockSpec((1, 1, count, size), lambda i, j, info: (0, half, block, 0)),
            pl.BlockSpec((1, 1, count, size), lambda i, j, info: (1, half, block, 0)),
            pl.BlockSpec((2 * size, tile), lambda i, j, info: (0, j)),
            pl.BlockSpec((1, tile), lambda i, j, info: (0, j)),
            pl.BlockSpec((count, tile), lambda i, j, info: (block, j)),
        ]
        operands += [reflectors, reflectors, s, scale, held]
        if out is not None:
            in_specs.append(pl.BlockSpec(memory_space=pl.ANY))
            operands.append(out)
            aliases = {len(operands): 0}
        out_shape = (2, held.shape[0], width)
        out_spec = pl.BlockSpec(
            (1, count, tile), lambda i, j, info: (half, block, jnp.where(i == pairs - 1, j, 0))
        )
        scratch += [pltpu.VMEM((count, 2 * size), jnp.bfloat16)] * 2
    if pairs > 1:
        scratch.append(pltpu.VMEM((width // tile, count, tile), jnp.float32))
    return pl.pallas_call(
        functools.partial(rows_kernel, (pairs, parts, rows), last),
        grid_spec=pltpu.PrefetchScalarGridSpec(
            num_scalar_prefetch=1,
            grid=(pairs, width // tile),
            in_specs=in_specs,
            out_specs=out_spec,
            scratch_shapes=scratch,
        ),
        out_shape=jax.ShapeDtypeStruct(out_shape, jnp.float32),
        input_output_aliases=aliases,
    )(info, *operands)


def project_kernel(y_ref, q_ref, o_ref, q_high, q_low):
    @pl.when(pl.program_id(1) == 0)
    def _():
        q_high[...], q_low[...] = split2(q_ref[0])

    o_ref[0] = dot3(*split2(y_ref[0, 0].T), q_high[...], q_low[...])


def project(reflectors, q_halves):
    _, rows, depth = q_halves.shape
    size = reflectors.shape[3]
    return pl.pallas_call(
        project_kernel,
        grid=(2, 2),
        in_specs=[
            pl.BlockSpec((1, 1, rows, size), lambda h, i: (i, h, 0, 0)),
            pl.BlockSpec((1, rows, depth), lambda h, i: (h, 0, 0)),
        ],
        out_specs=pl.BlockSpec((1, size, depth), lambda h, i: (h, i, 0)),
        out_shape=jax.ShapeDtypeStruct((2, 2 * size, depth), jnp.float32),
        scratch_shapes=[pltpu.VMEM((rows, depth), jnp.bfloat16)] * 2,
        name="project",
    )(reflectors, q_halves)


def merge(
    q_halves, pole_values, weights, secular_roots, column_order, deflated, reflectors, triangles
):
    col_count, row_count = lax.axis_size("col"), lax.axis_size("row")
    me, my_row = lax.axis_index("col"), lax.axis_index("row")
    _, rows, depth = q_halves.shape
    width = 2 * depth
    exact = dict(precision=lax.Precision.HIGHEST)
    cut = rows // 2

    def swap(x, mask):
        return lax.ppermute(x, "col", [(i, i ^ mask) for i in range(col_count)])

    def row_swap(x, mask):
        return lax.ppermute(x, "row", [(i, i ^ mask) for i in range(row_count)])

    bits = [1 << b for b in range(1, (col_count - 1).bit_length())]
    near = [0] + bits
    far = [m for m in range(2, col_count, 2) if m not in bits]

    partner = swap(q_halves, 1)
    got = [{} for _ in range(2)]
    for h in range(2):
        own = [q_halves[h, :cut], q_halves[h, cut:]]
        for bit in bits:
            order = (1, 0) if bit == bits[0] else (0, 1)
            parts = {p: swap(own[p], bit) for p in order}
            got[h][bit] = [parts[0], parts[1]]
    for h in range(2):
        for m in far:
            set_bits = [b for b in bits if b & m]
            via = [set_bits[0], set_bits[-1]]
            got[h][m] = [swap(got[h][m ^ via[p]][p], via[p]) for p in range(2)]
        for m in bits + far:
            got[h][m + 1] = [swap(x, 1) for x in got[h][m]]

    r_part = project(reflectors, q_halves)
    share = r_part.shape[1] // row_count
    r_mine = lax.dynamic_slice_in_dim(r_part, my_row * share, share, axis=1)
    for m in range(1, row_count):
        away = lax.dynamic_slice_in_dim(r_part, (my_row ^ m) * share, share, axis=1)
        r_mine = r_mine + row_swap(away, m)
    r_all = lax.all_gather(r_mine, "col", axis=2, tiled=True)
    cross = lax.psum(jnp.einsum("hrb,hrd->bd", reflectors[0], reflectors[1], **exact), "row")

    zeds = weights * (1 - deflated).astype(jnp.float32)
    source = lax.dynamic_slice_in_dim(column_order, me * width, width)
    roots = jnp.take(jnp.where(deflated > 0, FAR, secular_roots), source)
    gone = roots > 1e38
    keys = jnp.where(gone, source, -1)
    c_high, c_low, total = make_cauchy(pole_values, zeds, roots, keys)
    scale = jnp.where(gone[None, :], 1.0, lax.rsqrt(total + EPSILON))

    def pieces_of(h, masks, parts):
        pieces = []
        for m in masks:
            if m == 0:
                pieces.append([[q_halves] * len(parts), [partner] * len(parts)])
            else:
                pieces.append([[got[h][m + k][p] for p in parts] for k in range(2)])
        return pieces

    held = []
    for h in range(2):
        held.append(rows_call(h, 0, near, pieces_of(h, near, (0, 1)), c_high, c_low))

    p_part = early_projection(r_all, c_high, c_low)
    p_stack = jnp.stack([p_part] + [row_swap(p_part, m) for m in range(1, row_count)])
    p_all = jnp.concatenate(
        [lax.dynamic_index_in_dim(p_stack, my_row ^ z, keepdims=False) for z in range(row_count)]
    )
    size = triangles.shape[1]
    upper = jnp.triu(triangles)
    s1 = jnp.dot(upper[1], p_all[size:], **exact)
    s0 = jnp.dot(upper[0], p_all[:size] - jnp.dot(cross, s1, **exact), **exact)
    s = jnp.concatenate([s0, s1], axis=0)

    out = None
    for h in range(2):
        for block, parts in [(0, (0, 1))] if h == 0 else [(0, (0,)), (1, (1,))]:
            out = rows_call(
                h, block, far, pieces_of(h, far, parts), c_high, c_low,
                (reflectors, s, scale, held[h], out),
            )
    return out


def solution(mesh):
    placed = (P(None, "row", "col"), P(), P(), P(), P(), P(), P(None, None, "row", None), P())
    return jax.shard_map(
        merge, mesh=mesh, in_specs=placed, out_specs=P(None, "row", "col"), check_vma=False
    )
```

profile of v0, /device:TPU:0, one launch (start us, length us, event | category | flops | bytes accessed | tf_op | source)
XLA Modules:
  0.0 604.3 jit_solution(2898191476015193212)
XLA Ops:
  7.4 12.1 %project.1 = f32[2,512,640]{2,1,0:T(8,128)} custom-call(f32[2,2,1280,256]{3,2,1,0:T(8,128)} %refs_5_.3, f32[2,1280,640]{2,1,0:T(8,128)} %refs_1_.3), custom_call_target="tpu_custom_call" | custom-call | tf_op jit(solution)/shard_map/project/pallas_call | solution.py:234
  19.5 1.6 constant_dynamic-slice_fusion.2
  21.1 3.1 collective-permute-start.3
  24.2 2.6 collective-permute-start.4
  26.8 25.4 %collective-permute-done.3 = f32[2,128,640]{2,1,0:T(8,128)S(1)} collective-permute-done((f32[2,128,640]{2,1,0:T(8,128)S(1)}, f32[2,128,640]{2,1,0:T(8,128)S(1)}, u32[]{:S(2)}, u32[]{:S(2)}) %collective-permute-start.3) | collective-permute-done | bytes 655392 | tf_op jit(solution)/shard_map/ppermute | solution.py:262
  52.3 18.6 %collective-permute-done.4 = f32[2,128,640]{2,1,0:T(8,128)S(1)} collective-permute-done((f32[2,128,640]{2,1,0:T(8,128)S(1)}, f32[2,128,640]{2,1,0:T(8,128)S(1)}, u32[]{:S(2)}, u32[]{:S(2)}) %collective-permute-start.4) | collective-permute-done | bytes 655392 | tf_op jit(solution)/shard_map/ppermute | solution.py:262
  70.8 2.3 add_add_fusion
  73.2 3.4 slice_bitcast_fusion
  76.5 1.6 collective-permute-start.21
  78.1 1.5 collective-permute-start.19
  79.6 0.5 collective-permute-start.25
  80.2 0.5 collective-permute-start.28
  80.7 1.5 collective-permute-start
  82.2 45.0 %collective-permute-done.21.refs_5_ = f32[640,640]{1,0:T(8,128)S(1)} collective-permute-done((f32[640,640]{1,0:T(8,128)S(1)}, f32[640,640]{1,0:T(8,128)S(1)}, u32[]{:S(2)}, u32[]{:S(2)}) %collective-permute-start.21) | collective-permute-done | bytes 1638432 | tf_op jit(solution)/shard_map/ppermute | solution.py:259
  127.2 1.4 collective-permute-start.13
  128.6 1.6 collective-permute-done.19.refs_8_
  130.2 41.2 %collective-permute-done.25.refs_4_ = f32[640,640]{1,0:T(8,128)S(1)} collective-permute-done((f32[640,640]{1,0:T(8,128)S(1)}, f32[640,640]{1,0:T(8,128)S(1)}, u32[]{:S(2)}, u32[]{:S(2)}) %collective-permute-start.25) | collective-permute-done | bytes 1638432 | tf_op jit(solution)/shard_map/ppermute | solution.py:259
  171.5 1.5 collective-permute-start.10
  173.0 1.5 collective-permute-start.14
  174.5 32.1 %collective-permute-done.refs_5_ = f32[640,640]{1,0:T(8,128)S(1)} collective-permute-done((f32[640,640]{1,0:T(8,128)S(1)}, f32[640,640]{1,0:T(8,128)S(1)}, u32[]{:S(2)}, u32[]{:S(2)}) %collective-permute-start) | collective-permute-done | bytes 1638432 | tf_op jit(solution)/shard_map/ppermute | solution.py:259
  206.6 1.6 collective-permute-done.13.refs_8_
  208.2 30.2 %collective-permute-done.10.refs_4_ = f32[640,640]{1,0:T(8,128)} collective-permute-done((f32[640,640]{1,0:T(8,128)S(1)}, f32[640,640]{1,0:T(8,128)}, u32[]{:S(2)}, u32[]{:S(2)}) %collective-permute-start.10) | collective-permute-done | bytes 1638432 | tf_op jit(solution)/shard_map/ppermute | solution.py:259
  238.4 1.2 collective-permute-done.14.refs_9_
  239.6 0.8 collective-permute-start.20
  240.4 1.5 collective-permute-start.22
  242.0 2.2 collective-permute-done.30.refs_11_
  244.2 0.1 collective-permute-start.15
  244.3 33.6 %collective-permute-done.20.refs_0_ = f32[640,640]{1,0:T(8,128)} collective-permute-done((f32[640,640]{1,0:T(8,128)S(1)}, f32[640,640]{1,0:T(8,128)}, u32[]{:S(2)}, u32[]{:S(2)}) %collective-permute-start.20) | collective-permute-done | bytes 1638432 | tf_op jit(solution)/shard_map/ppermute | solution.py:259
  277.9 0.2 collective-permute-done.22.refs_1_
  278.2 0.3 collective-permute-start.16
  278.5 7.5 %fusion.9 = f32[256,256]{1,0:T(8,128)} fusion(f32[2,2,1280,256]{3,2,1,0:T(8,128)} %refs_5_.3), kind=kOutput, calls=%fused_computation.17 | convolution fusion | flops 2013265920 | bytes 5505024 | tf_op jit(solution)/shard_map/hrb,hrd->bd/dot_general | solution.py:291
  286.1 1.3 collective-permute-start.17
  287.4 1.5 collective-permute-start.1
  288.9 0.8 compare_select_fusion.1
  289.7 7.5 %gather_fusion = f32[1280]{0:T(1024)S(1)} fusion(f32[10240]{0:T(1024)S(1)} %get-tuple-element.25, s32[2048]{0:T(1024)S(1)} %pad_clamp_fusion), kind=kCustom, calls=%fused_computation | custom fusion | bytes 15360 | tf_op jit(solution)/shard_map/jit(_take)/gather | solution.py:295
  297.3 0.8 dynamic-slice_select_fusion
  298.1 0.6 broadcast_in_dim.45.key_ref
  298.7 0.6 select_n.62.root_ref
  299.3 3.1 copy.12.zed_ref
  302.3 3.1 copy.11.pole_ref
  305.5 40.5 %cauchy.1 = (bf16[10240,1280]{1,0:T(8,128)(2,1)}, bf16[10240,1280]{1,0:T(8,128)(2,1)}, f32[1,1280]{1,0:T(1,128)}) custom-call(f32[10240,1]{1,0:T(8,128)} %copy.11.pole_ref, f32[10240,1]{1,0:T(8,128)} %copy.12.zed_ref, f32[1,1280]{1,0:T(1,128)} %select_n.62.root_ref, s32[1,1280]{1,0:T(1,128)} %broadcast_in_dim.45.key_ref), custom_call_target="tpu_custom_call" | custom-call | tf_op jit(solution)/shard_map/cauchy/pallas_call | solution.py:47
  345.9 0.6 stack.80.info_ref
  346.5 0.7 stack.73.info_ref
  347.2 0.7 pad_add_fusion.info_ref
  347.8 0.6 add_add_fusion.1
  348.5 0.1 iota_compare_fusion
  348.6 29.4 %early.1 = f32[128,1280]{1,0:T(8,128)} custom-call(f32[2,128,5120]{2,1,0:T(8,128)} %all-gather.2.cloned.1.call-done.r_ref, bf16[10240,1280]{1,0:T(8,128)(2,1)} %get-tuple-element.8.ch_ref.refs_12_.refs_4_.refs_2_, bf16[10240,1280]{1,0:T(8,128)(2,1)} %get-tuple-element.9.cl_ref.refs_13_.refs_5_.refs_3_), custom_call_target="tpu_custom_call" | custom-call | tf_op jit(solution)/shard_map/early/pallas_call | solution.py:72
  378.0 14.6 %collective-permute-start.6 = (f32[128,1280]{1,0:T(8,128)}, f32[128,1280]{1,0:T(8,128)}, u32[]{:S(2)}, u32[]{:S(2)}) collective-permute-start(f32[128,1280]{1,0:T(8,128)} %early.1), channel_id=1, source_target_pairs={{0,8},{8,0},{16,24},{24,16},{1,9},{9,1},{17,25},{25,17},{2,10},{10... | collective-permute-start | bytes 1966088 | tf_op jit(solution)/shard_map/ppermute | solution.py:262
  392.6 1.1 collective-permute-start.7
  393.7 1.5 collective-permute-start.8
  395.2 0.6 reshape_select_fusion.refs_9_.refs_7_
  395.8 53.6 %shard_map.83.refs_10_ = f32[1280,1280]{1,0:T(8,128)} custom-call(s32[6]{0:T(128)} %stack.80.info_ref, f32[2,1280,640]{2,1,0:T(8,128)} %refs_1_.3, f32[2,1280,640]{2,1,0:T(8,128)} %refs_1_.3, f32[2,1280,640]{2,1,0:T(8,128)} %collective-permute-done.9.refs_2_.refs_3_, f32[2,1280,640]{2,1,0:T(8,128)} %collective-permute-done.9.refs_2_.refs_3_, ...), custom_call_target="tpu_custom_call" | custom-call | tf_op jit(solution)/shard_map/pallas_call | solution.py:209
  449.4 53.9 %shard_map.82.refs_8_ = f32[1280,1280]{1,0:T(8,128)} custom-call(s32[6]{0:T(128)} %stack.73.info_ref, f32[2,1280,640]{2,1,0:T(8,128)} %refs_1_.3, f32[2,1280,640]{2,1,0:T(8,128)} %refs_1_.3, f32[2,1280,640]{2,1,0:T(8,128)} %collective-permute-done.9.refs_2_.refs_3_, f32[2,1280,640]{2,1,0:T(8,128)} %collective-permute-done.9.refs_2_.refs_3_, ...), custom_call_target="tpu_custom_call" | custom-call | tf_op jit(solution)/shard_map/pallas_call | solution.py:209
  503.4 0.5 collective-permute-start.24
  504.0 0.4 collective-permute-start.2
  504.4 1.7 pad_maximum_fusion
  506.1 0.3 dynamic-slice_bitcast_fusion.3
  506.4 1.2 fusion.5
  507.7 2.2 convolution_subtract_fusion
  509.9 1.3 fusion.14
  511.2 1.7 pad_maximum_fusion.1.refs_8_.refs_6_
  512.9 39.1 %shard_map.84.refs_9_ = f32[2,1280,1280]{2,1,0:T(8,128)} custom-call(s32[4]{0:T(128)} %pad_add_fusion.info_ref, f32[640,640]{1,0:T(8,128)} %collective-permute-done.20.refs_0_, f32[640,640]{1,0:T(8,128)} %collective-permute-done.22.refs_1_, f32[640,640]{1,0:T(8,128)} %collective-permute-done.23.refs_2_, f32[640,640]{1,0:T(8,128)} %collective-permute-done.24.refs_3_, ...), custom_call_target="tpu_custom_call" | custom-call | tf_op jit(solution)/shard_map/pallas_call | solution.py:209
  552.0 22.3 %shard_map.85.refs_9_ = f32[2,1280,1280]{2,1,0:T(8,128)} custom-call(s32[4]{0:T(128)} %get-tuple-element.28.info_ref, f32[640,640]{1,0:T(8,128)} %collective-permute-done.17.refs_0_, f32[640,640]{1,0:T(8,128)} %collective-permute-done.18.refs_1_, ...), custom_call_target="tpu_custom_call", output_to_operand_aliasing={{}: (10, {})} | custom-call | tf_op jit(solution)/shard_map/pallas_call | solution.py:209
  574.3 22.3 %shard_map.86 = f32[2,1280,1280]{2,1,0:T(8,128)} custom-call(s32[4]{0:T(128)} %get-tuple-element.27.info_ref, f32[640,640]{1,0:T(8,128)} %collective-permute-done.1.refs_0_, f32[640,640]{1,0:T(8,128)} %collective-permute-done.2.refs_1_, bf16[10240,1280]{1,0:T(8,128)(2,1)} %get-tuple-element.8.ch_ref.refs_12_.refs_4_.refs_2_, ...), custom_call_target="tpu_custom_call", output_to_operand_aliasing={{}: (10, {})} | custom-call | tf_op jit(solution)/shard_map/pallas_call | solution.py:209
  (73 shorter events, 0.6 us)
Async XLA Ops:
  7.4 341.2 %all-gather.2.cloned.1.call-start = ((), (), s32[]{:S(2)}) async-start(), calls=%async_computation | async-start | bytes 5898240 | tf_op jit(solution)/shard_map/all_gather | solution.py:290
  21.1 31.1 %collective-permute-start.3 = (f32[2,128,640]{2,1,0:T(8,128)S(1)}, f32[2,128,640]{2,1,0:T(8,128)S(1)}, u32[]{:S(2)}, u32[]{:S(2)}) collective-permute-start(f32[2,128,640]{2,1,0:T(8,128)S(1)} %get-tuple-element.22), channel_id=1, source_target_pairs={{0,8},{8,0},{16,24},{24,16},{1,9},{9,1},{17,25},{25,17},{2,10},{10... | collective-permute-start | bytes 1966088 | tf_op jit(solution)/shard_map/ppermute | solution.py:262
  24.2 46.6 %collective-permute-start.4 = (f32[2,128,640]{2,1,0:T(8,128)S(1)}, f32[2,128,640]{2,1,0:T(8,128)S(1)}, u32[]{:S(2)}, u32[]{:S(2)}) collective-permute-start(f32[2,128,640]{2,1,0:T(8,128)S(1)} %get-tuple-element.24), channel_id=1, source_target_pairs={{0,16},{8,24},{16,0},{24,8},{1,17},{9,25},{17,1},{25,9},{2,18},{10... | collective-permute-start | bytes 1966088 | tf_op jit(solution)/shard_map/ppermute | solution.py:262
  26.8 44.0 %collective-permute-start.5 = (f32[2,128,640]{2,1,0:T(8,128)S(1)}, f32[2,128,640]{2,1,0:T(8,128)}, u32[]{:S(2)}, u32[]{:S(2)}) collective-permute-start(f32[2,128,640]{2,1,0:T(8,128)S(1)} %get-tuple-element.23), channel_id=1, source_target_pairs={{0,24},{8,16},{16,8},{24,0},{1,25},{9,17},{17,9},{25,1},{2,26},{10... | collective-permute-start | bytes 1966088 | tf_op jit(solution)/shard_map/ppermute | solution.py:262
  73.1 434.6 %all-reduce.2.cloned.1.call-start = ((), (), s32[]{:S(2)}) async-start(), calls=%async_computation.1 | async-start | bytes 524288 | tf_op jit(solution)/shard_map/psum | solution.py:291
  76.5 50.6 %collective-permute-start.21 = (f32[640,640]{1,0:T(8,128)S(1)}, f32[640,640]{1,0:T(8,128)S(1)}, u32[]{:S(2)}, u32[]{:S(2)}) collective-permute-start(f32[640,640]{1,0:T(8,128)S(1)} %get-tuple-element.14), channel_id=1, source_target_pairs={{0,2},{1,3},{2,0},{3,1},{4,6},{5,7},{6,4},{7,5},{8,10},{9,11},{10,... | collective-permute-start | bytes 4915208 | tf_op jit(solution)/shard_map/ppermute | solution.py:259
  78.1 52.1 %collective-permute-start.19 = (f32[640,640]{1,0:T(8,128)S(1)}, f32[640,640]{1,0:T(8,128)S(1)}, u32[]{:S(2)}, u32[]{:S(2)}) collective-permute-start(f32[640,640]{1,0:T(8,128)S(1)} %get-tuple-element.15), channel_id=1, source_target_pairs={{0,4},{1,5},{2,6},{3,7},{4,0},{5,1},{6,2},{7,3},{8,12},{9,13},{10,... | collective-permute-start | bytes 4915208 | tf_op jit(solution)/shard_map/ppermute | solution.py:259
  79.6 91.8 %collective-permute-start.25 = (f32[640,640]{1,0:T(8,128)S(1)}, f32[640,640]{1,0:T(8,128)S(1)}, u32[]{:S(2)}, u32[]{:S(2)}) collective-permute-start(f32[640,640]{1,0:T(8,128)S(1)} %get-tuple-element.15), channel_id=1, source_target_pairs={{0,2},{1,3},{2,0},{3,1},{4,6},{5,7},{6,4},{7,5},{8,10},{9,11},{10,... | collective-permute-start | bytes 4915208 | tf_op jit(solution)/shard_map/ppermute | solution.py:259
  80.2 92.8 %collective-permute-start.28 = (f32[640,640]{1,0:T(8,128)S(1)}, f32[640,640]{1,0:T(8,128)S(1)}, u32[]{:S(2)}, u32[]{:S(2)}) collective-permute-start(f32[640,640]{1,0:T(8,128)S(1)} %get-tuple-element.14), channel_id=1, source_target_pairs={{0,4},{1,5},{2,6},{3,7},{4,0},{5,1},{6,2},{7,3},{8,12},{9,13},{10,... | collective-permute-start | bytes 4915208 | tf_op jit(solution)/shard_map/ppermute | solution.py:259
  80.7 125.9 %collective-permute-start = (f32[640,640]{1,0:T(8,128)S(1)}, f32[640,640]{1,0:T(8,128)S(1)}, u32[]{:S(2)}, u32[]{:S(2)}) collective-permute-start(f32[640,640]{1,0:T(8,128)S(1)} %get-tuple-element.17), channel_id=1, source_target_pairs={{0,2},{1,3},{2,0},{3,1},{4,6},{5,7},{6,4},{7,5},{8,10},{9,11},{10,... | collective-permute-start | bytes 4915208 | tf_op jit(solution)/shard_map/ppermute | solution.py:259
  127.2 114.7 %copy-start.2 = (f32[640,640]{1,0:T(8,128)}, f32[640,640]{1,0:T(8,128)S(1)}, u32[]{:S(2)}) copy-start(f32[640,640]{1,0:T(8,128)S(1)} %collective-permute-done.21.refs_5_) | copy-start | bytes 4915204
  127.2 158.8 %copy-start.12 = (f32[10240]{0:T(1024)S(1)}, f32[10240]{0:T(1024)}, u32[]{:S(2)}) copy-start(f32[10240]{0:T(1024)} %param.11) | copy-start | bytes 122884
  127.2 158.9 %copy-start.13 = (s32[10240]{0:T(1024)S(1)}, s32[10240]{0:T(1024)}, u32[]{:S(2)}) copy-start(s32[10240]{0:T(1024)} %param.13) | copy-start | bytes 122884
  127.2 158.9 %copy-start.14 = (f32[10240]{0:T(1024)S(1)}, f32[10240]{0:T(1024)}, u32[]{:S(2)}) copy-start(f32[10240]{0:T(1024)} %param.10) | copy-start | bytes 122884
  127.2 81.0 %collective-permute-start.13 = (f32[640,640]{1,0:T(8,128)S(1)}, f32[640,640]{1,0:T(8,128)}, u32[]{:S(2)}, u32[]{:S(2)}) collective-permute-start(f32[640,640]{1,0:T(8,128)S(1)} %get-tuple-element.16), channel_id=1, source_target_pairs={{0,4},{1,5},{2,6},{3,7},{4,0},{5,1},{6,2},{7,3},{8,12},{9,13},{10,... | collective-permute-start | bytes 4915208 | tf_op jit(solution)/shard_map/ppermute | solution.py:259
  130.2 147.9 %copy-start.3 = (f32[640,640]{1,0:T(8,128)}, f32[640,640]{1,0:T(8,128)S(1)}, u32[]{:S(2)}) copy-start(f32[640,640]{1,0:T(8,128)S(1)} %collective-permute-done.19.refs_8_) | copy-start | bytes 4915204
  130.2 263.5 %collective-permute-start.9 = (f32[2,1280,640]{2,1,0:T(8,128)}, f32[2,1280,640]{2,1,0:T(8,128)}, u32[]{:S(2)}, u32[]{:S(2)}) collective-permute-start(f32[2,1280,640]{2,1,0:T(8,128)} %refs_1_.3), channel_id=1, source_target_pairs={{0,1},{1,0},{2,3},{3,2},{4,5},{5,4},{6,7},{7,6},{8,9},{9,8},{10,11... | collective-permute-start | bytes 19660808 | tf_op jit(solution)/shard_map/ppermute | solution.py:259
  171.5 107.0 %copy-start.4 = (f32[640,640]{1,0:T(8,128)}, f32[640,640]{1,0:T(8,128)S(1)}, u32[]{:S(2)}) copy-start(f32[640,640]{1,0:T(8,128)S(1)} %collective-permute-done.25.refs_4_) | copy-start | bytes 4915204
  171.5 66.9 %collective-permute-start.10 = (f32[640,640]{1,0:T(8,128)S(1)}, f32[640,640]{1,0:T(8,128)}, u32[]{:S(2)}, u32[]{:S(2)}) collective-permute-start(f32[640,640]{1,0:T(8,128)S(1)} %get-tuple-element.16), channel_id=1, source_target_pairs={{0,2},{1,3},{2,0},{3,1},{4,6},{5,7},{6,4},{7,5},{8,10},{9,11},{10,... | collective-permute-start | bytes 4915208 | tf_op jit(solution)/shard_map/ppermute | solution.py:259
  173.0 105.5 %copy-start.5 = (f32[640,640]{1,0:T(8,128)}, f32[640,640]{1,0:T(8,128)S(1)}, u32[]{:S(2)}) copy-start(f32[640,640]{1,0:T(8,128)S(1)} %collective-permute-done.28.refs_9_) | copy-start | bytes 4915204
  173.0 66.6 %collective-permute-start.14 = (f32[640,640]{1,0:T(8,128)S(1)}, f32[640,640]{1,0:T(8,128)}, u32[]{:S(2)}, u32[]{:S(2)}) collective-permute-start(f32[640,640]{1,0:T(8,128)S(1)} %get-tuple-element.17), channel_id=1, source_target_pairs={{0,4},{1,5},{2,6},{3,7},{4,0},{5,1},{6,2},{7,3},{8,12},{9,13},{10,... | collective-permute-start | bytes 4915208 | tf_op jit(solution)/shard_map/ppermute | solution.py:259
  206.6 80.8 %copy-start.1 = (f32[640,640]{1,0:T(8,128)}, f32[640,640]{1,0:T(8,128)S(1)}, u32[]{:S(2)}) copy-start(f32[640,640]{1,0:T(8,128)S(1)} %collective-permute-done.refs_5_) | copy-start | bytes 4915204
  206.6 33.0 %collective-permute-start.27 = (f32[640,640]{1,0:T(8,128)S(1)}, f32[640,640]{1,0:T(8,128)S(1)}, u32[]{:S(2)}, u32[]{:S(2)}) collective-permute-start(f32[640,640]{1,0:T(8,128)S(1)} %collective-permute-done.21.refs_5_), channel_id=1, source_target_pairs={{0,1},{1,0},{2,3},{3,2},{4,5},{5,4},{6,7},{7,6},{8,9},{9,8},{10,11... | collective-permute-start | bytes 4915208 | tf_op jit(solution)/shard_map/ppermute | solution.py:259
  208.2 32.2 %collective-permute-start.29 = (f32[640,640]{1,0:T(8,128)S(1)}, f32[640,640]{1,0:T(8,128)S(1)}, u32[]{:S(2)}, u32[]{:S(2)}) collective-permute-start(f32[640,640]{1,0:T(8,128)S(1)} %collective-permute-done.19.refs_8_), channel_id=1, source_target_pairs={{0,1},{1,0},{2,3},{3,2},{4,5},{5,4},{6,7},{7,6},{8,9},{9,8},{10,11... | collective-permute-start | bytes 4915208 | tf_op jit(solution)/shard_map/ppermute | solution.py:259
  238.4 3.5 collective-permute-start.26
  239.6 4.6 collective-permute-start.30
  239.6 38.8 %copy-start.6 = (f32[640,640]{1,0:T(8,128)}, f32[640,640]{1,0:T(8,128)S(1)}, u32[]{:S(2)}) copy-start(f32[640,640]{1,0:T(8,128)S(1)} %collective-permute-done.27.refs_7_) | copy-start | bytes 4915204
  239.6 38.3 %collective-permute-start.20 = (f32[640,640]{1,0:T(8,128)S(1)}, f32[640,640]{1,0:T(8,128)}, u32[]{:S(2)}, u32[]{:S(2)}) collective-permute-start(f32[640,640]{1,0:T(8,128)S(1)} %collective-permute-done.19.refs_8_), channel_id=1, source_target_pairs={{0,2},{1,3},{2,0},{3,1},{4,6},{5,7},{6,4},{7,5},{8,10},{9,11},{10,... | collective-permute-start | bytes 4915208 | tf_op jit(solution)/shard_map/ppermute | solution.py:259
  240.4 38.1 %copy-start.7 = (f32[640,640]{1,0:T(8,128)}, f32[640,640]{1,0:T(8,128)S(1)}, u32[]{:S(2)}) copy-start(f32[640,640]{1,0:T(8,128)S(1)} %collective-permute-done.29.refs_10_) | copy-start | bytes 4915204
  240.4 37.8 %collective-permute-start.22 = (f32[640,640]{1,0:T(8,128)S(1)}, f32[640,640]{1,0:T(8,128)}, u32[]{:S(2)}, u32[]{:S(2)}) collective-permute-start(f32[640,640]{1,0:T(8,128)S(1)} %collective-permute-done.21.refs_5_), channel_id=1, source_target_pairs={{0,4},{1,5},{2,6},{3,7},{4,0},{5,1},{6,2},{7,3},{8,12},{9,13},{10,... | collective-permute-start | bytes 4915208 | tf_op jit(solution)/shard_map/ppermute | solution.py:259
  241.9 36.5 %copy-start.8 = (f32[640,640]{1,0:T(8,128)}, f32[640,640]{1,0:T(8,128)S(1)}, u32[]{:S(2)}) copy-start(f32[640,640]{1,0:T(8,128)S(1)} %collective-permute-done.26.refs_6_) | copy-start | bytes 4915204
  241.9 44.2 %collective-permute-start.12 = (f32[640,640]{1,0:T(8,128)S(1)}, f32[640,640]{1,0:T(8,128)}, u32[]{:S(2)}, u32[]{:S(2)}) collective-permute-start(f32[640,640]{1,0:T(8,128)S(1)} %collective-permute-done.refs_5_), channel_id=1, source_target_pairs={{0,1},{1,0},{2,3},{3,2},{4,5},{5,4},{6,7},{7,6},{8,9},{9,8},{10,11... | collective-permute-start | bytes 4915208 | tf_op jit(solution)/shard_map/ppermute | solution.py:259
  244.2 34.2 %copy-start.9 = (f32[640,640]{1,0:T(8,128)}, f32[640,640]{1,0:T(8,128)S(1)}, u32[]{:S(2)}) copy-start(f32[640,640]{1,0:T(8,128)S(1)} %collective-permute-done.30.refs_11_) | copy-start | bytes 4915204
  244.2 43.2 %collective-permute-start.15 = (f32[640,640]{1,0:T(8,128)}, f32[640,640]{1,0:T(8,128)}, u32[]{:S(2)}, u32[]{:S(2)}) collective-permute-start(f32[640,640]{1,0:T(8,128)} %collective-permute-done.13.refs_8_), channel_id=1, source_target_pairs={{0,1},{1,0},{2,3},{3,2},{4,5},{5,4},{6,7},{7,6},{8,9},{9,8},{10,11... | collective-permute-start | bytes 4915208 | tf_op jit(solution)/shard_map/ppermute | solution.py:259
  277.9 100.1 %collective-permute-start.11 = (f32[640,640]{1,0:T(8,128)}, f32[640,640]{1,0:T(8,128)}, u32[]{:S(2)}, u32[]{:S(2)}) collective-permute-start(f32[640,640]{1,0:T(8,128)} %collective-permute-done.10.refs_4_), channel_id=1, source_target_pairs={{0,1},{1,0},{2,3},{3,2},{4,5},{5,4},{6,7},{7,6},{8,9},{9,8},{10,11... | collective-permute-start | bytes 4915208 | tf_op jit(solution)/shard_map/ppermute | solution.py:259
  278.2 114.4 %collective-permute-start.16 = (f32[640,640]{1,0:T(8,128)}, f32[640,640]{1,0:T(8,128)}, u32[]{:S(2)}, u32[]{:S(2)}) collective-permute-start(f32[640,640]{1,0:T(8,128)} %collective-permute-done.14.refs_9_), channel_id=1, source_target_pairs={{0,1},{1,0},{2,3},{3,2},{4,5},{5,4},{6,7},{7,6},{8,9},{9,8},{10,11... | collective-permute-start | bytes 4915208 | tf_op jit(solution)/shard_map/ppermute | solution.py:259
  286.1 217.2 %collective-permute-start.17 = (f32[640,640]{1,0:T(8,128)}, f32[640,640]{1,0:T(8,128)}, u32[]{:S(2)}, u32[]{:S(2)}) collective-permute-start(f32[640,640]{1,0:T(8,128)} %collective-permute-done.13.refs_8_), channel_id=1, source_target_pairs={{0,2},{1,3},{2,0},{3,1},{4,6},{5,7},{6,4},{7,5},{8,10},{9,11},{10,... | collective-permute-start | bytes 4915208 | tf_op jit(solution)/shard_map/ppermute | solution.py:259
  287.4 216.0 %collective-permute-start.1 = (f32[640,640]{1,0:T(8,128)S(1)}, f32[640,640]{1,0:T(8,128)}, u32[]{:S(2)}, u32[]{:S(2)}) collective-permute-start(f32[640,640]{1,0:T(8,128)S(1)} %collective-permute-done.refs_5_), channel_id=1, source_target_pairs={{0,4},{1,5},{2,6},{3,7},{4,0},{5,1},{6,2},{7,3},{8,12},{9,13},{10,... | collective-permute-start | bytes 4915208 | tf_op jit(solution)/shard_map/ppermute | solution.py:259
  299.3 3.1 copy-start.11
  348.6 46.6 %copy-start.10 = (f32[2,256,256]{2,1,0:T(8,128)S(1)}, f32[2,256,256]{2,1,0:T(8,128)}, u32[]{:S(2)}) copy-start(f32[2,256,256]{2,1,0:T(8,128)} %param.15) | copy-start | bytes 1572868
  348.6 46.6 %copy-start.15 = (f32[1,1280]{1,0:T(1,128)S(1)}, f32[1,1280]{1,0:T(1,128)}, u32[]{:S(2)}) copy-start(f32[1,1280]{1,0:T(1,128)} %get-tuple-element.10) | copy-start | bytes 15364
  378.0 125.8 %collective-permute-start.6 = (f32[128,1280]{1,0:T(8,128)}, f32[128,1280]{1,0:T(8,128)}, u32[]{:S(2)}, u32[]{:S(2)}) collective-permute-start(f32[128,1280]{1,0:T(8,128)} %early.1), channel_id=1, source_target_pairs={{0,8},{8,0},{16,24},{24,16},{1,9},{9,1},{17,25},{25,17},{2,10},{10... | collective-permute-start | bytes 1966088 | tf_op jit(solution)/shard_map/ppermute | solution.py:262
  392.6 111.4 %collective-permute-start.7 = (f32[128,1280]{1,0:T(8,128)}, f32[128,1280]{1,0:T(8,128)}, u32[]{:S(2)}, u32[]{:S(2)}) collective-permute-start(f32[128,1280]{1,0:T(8,128)} %early.1), channel_id=1, source_target_pairs={{0,16},{8,24},{16,0},{24,8},{1,17},{9,25},{17,1},{25,9},{2,18},{10... | collective-permute-start | bytes 1966088 | tf_op jit(solution)/shard_map/ppermute | solution.py:262
  393.7 110.7 %collective-permute-start.8 = (f32[128,1280]{1,0:T(8,128)}, f32[128,1280]{1,0:T(8,128)}, u32[]{:S(2)}, u32[]{:S(2)}) collective-permute-start(f32[128,1280]{1,0:T(8,128)} %early.1), channel_id=1, source_target_pairs={{0,24},{8,16},{16,8},{24,0},{1,25},{9,17},{17,9},{25,1},{2,26},{10... | collective-permute-start | bytes 1966088 | tf_op jit(solution)/shard_map/ppermute | solution.py:262
  449.4 55.0 %copy-start = (f32[128,1280]{1,0:T(8,128)S(1)}, f32[128,1280]{1,0:T(8,128)}, u32[]{:S(2)}) copy-start(f32[128,1280]{1,0:T(8,128)} %early.1) | copy-start | bytes 1966084
  503.3 9.6 %collective-permute-start.23 = (f32[640,640]{1,0:T(8,128)}, f32[640,640]{1,0:T(8,128)}, u32[]{:S(2)}, u32[]{:S(2)}) collective-permute-start(f32[640,640]{1,0:T(8,128)} %collective-permute-done.20.refs_0_), channel_id=1, source_target_pairs={{0,1},{1,0},{2,3},{3,2},{4,5},{5,4},{6,7},{7,6},{8,9},{9,8},{10,11... | collective-permute-start | bytes 4915208 | tf_op jit(solution)/shard_map/ppermute | solution.py:259
  503.4 9.5 %collective-permute-start.24 = (f32[640,640]{1,0:T(8,128)}, f32[640,640]{1,0:T(8,128)}, u32[]{:S(2)}, u32[]{:S(2)}) collective-permute-start(f32[640,640]{1,0:T(8,128)} %collective-permute-done.22.refs_1_), channel_id=1, source_target_pairs={{0,1},{1,0},{2,3},{3,2},{4,5},{5,4},{6,7},{7,6},{8,9},{9,8},{10,11... | collective-permute-start | bytes 4915208 | tf_op jit(solution)/shard_map/ppermute | solution.py:259
  503.9 48.1 %collective-permute-start.18 = (f32[640,640]{1,0:T(8,128)}, f32[640,640]{1,0:T(8,128)}, u32[]{:S(2)}, u32[]{:S(2)}) collective-permute-start(f32[640,640]{1,0:T(8,128)} %collective-permute-done.17.refs_0_), channel_id=1, source_target_pairs={{0,1},{1,0},{2,3},{3,2},{4,5},{5,4},{6,7},{7,6},{8,9},{9,8},{10,11... | collective-permute-start | bytes 4915208 | tf_op jit(solution)/shard_map/ppermute | solution.py:259
  504.0 70.4 %collective-permute-start.2 = (f32[640,640]{1,0:T(8,128)}, f32[640,640]{1,0:T(8,128)}, u32[]{:S(2)}, u32[]{:S(2)}) collective-permute-start(f32[640,640]{1,0:T(8,128)} %collective-permute-done.1.refs_0_), channel_id=1, source_target_pairs={{0,1},{1,0},{2,3},{3,2},{4,5},{5,4},{6,7},{7,6},{8,9},{9,8},{10,11... | collective-permute-start | bytes 4915208 | tf_op jit(solution)/shard_map/ppermute | solution.py:259
Sparse Core Ops, SparseCore 0:
  73.2 74.1 all-gather.1
Sparse Core Ops, SparseCore 1:
  286.1 48.6 all-reduce.1
where the time goes:
time: 613 us; the launch traced here: 604 us
  Pallas kernels  273 us (45%)
  waiting for transfers between devices  233 us (38%)
  starting transfers between devices  39.6 us (6%)
  local copies, waits for them, and re-layouts  21.5 us (4%)
  between operations  15.4 us (3%)
  matrix products  12.3 us (2%)
  other arithmetic  9.32 us (2%)
    pallas_call x5, Pallas kernels, rows_call(): pl.pallas_call(functools.partial(rows_kernel, (pairs, parts, rows), last)...  191 us
    ppermute x25, waiting for transfers between devices, swap(): return lax.ppermute(x, 'col', [(i, i ^ mask) for i in range(col_count)])  189 us
    ppermute x6, waiting for transfers between devices, row_swap(): return lax.ppermute(x, 'row', [(i, i ^ mask) for i in range(row_count)])  44 us
    pallas_call x1, Pallas kernels, make_cauchy(): pl.pallas_call(cauchy_kernel, grid=(count // rows,), in_specs=[vec, vec,...  40.5 us
    pallas_call x1, Pallas kernels, early_projection(): pl.pallas_call(early_kernel, grid=(width // tile,), in_specs=[pl.BlockSpe...  29.4 us
    ppermute x6, starting transfers between devices, row_swap(): return lax.ppermute(x, 'row', [(i, i ^ mask) for i in range(row_count)])  22.8 us
    ppermute x25, starting transfers between devices, swap(): return lax.ppermute(x, 'col', [(i, i ^ mask) for i in range(col_count)])  16.8 us
  transfers between devices with their start and end apart: 33, of which 12 were waited for; matrix products, arithmetic and copies ran while one was open for 6% of the time, Pallas kernels for 40%

commit v1 on v0

--- a/solution.py
+++ b/solution.py
@@ -22,25 +22,33 @@
     return dot(a_high, b_high) + (dot(a_high, b_low) + dot(a_low, b_high))
 
 
-def cauchy_kernel(pole_ref, zed_ref, root_ref, key_ref, high_ref, low_ref, total_ref):
+def cauchy_kernel(pole_ref, zed_ref, root_ref, key_ref, high_ref, low_ref, total_ref, poles, zeds):
     step = pl.program_id(0)
-    rows = pole_ref.shape[0]
+    rows = high_ref.shape[0]
+    chunk = 256
 
     @pl.when(step == 0)
     def _():
         total_ref[...] = jnp.zeros_like(total_ref)
 
-    ratio = zed_ref[...] / (pole_ref[...] - root_ref[...])
-    total_ref[...] += jnp.sum(ratio * ratio, axis=0, keepdims=True)
-    row_ids = step * rows + lax.broadcasted_iota(jnp.int32, ratio.shape, 0)
-    value = jnp.where(row_ids == key_ref[...], 1.0, ratio)
-    high_ref[...], low_ref[...] = split2(value)
+    for ref, held in ((pole_ref, poles), (zed_ref, zeds)):
+        held[...] = jnp.broadcast_to(ref[...], (8, rows)).T
+
+    @pl.loop(0, rows // chunk)
+    def _(i):
+        at = pl.multiple_of(i * chunk, chunk)
+        span = pl.ds(at, chunk)
+        ratio = zeds[span, :1] / (poles[span, :1] - root_ref[...])
+        total_ref[...] += jnp.sum(ratio * ratio, axis=0, keepdims=True)
+        row_ids = step * rows + at + lax.broadcasted_iota(jnp.int32, ratio.shape, 0)
+        value = jnp.where(row_ids == key_ref[...], 1.0, ratio)
+        high_ref[span], low_ref[span] = split2(value)
 
 
 def make_cauchy(poles, zeds, roots, keys):
     count, width = poles.shape[0], roots.shape[0]
-    rows = 256
-    vec = pl.BlockSpec((rows, 1), lambda i: (i, 0))
+    rows = count // 8
+    vec = pl.BlockSpec((1, rows), lambda i: (0, i))
     line = pl.BlockSpec((1, width), lambda i: (0, 0))
     tile = pl.BlockSpec((rows, width), lambda i: (i, 0))
     part = jax.ShapeDtypeStruct((count, width), jnp.bfloat16)
@@ -50,8 +58,9 @@
         in_specs=[vec, vec, line, line],
         out_specs=[tile, tile, line],
         out_shape=[part, part, jax.ShapeDtypeStruct((1, width), jnp.float32)],
+        scratch_shapes=[pltpu.VMEM((rows, 8), jnp.float32)] * 2,
         name="cauchy",
-    )(poles[:, None], zeds[:, None], roots[None, :], keys[None, :])
+    )(poles[None, :], zeds[None, :], roots[None, :], keys[None, :])
 
 
 def early_kernel(r_ref, ch_ref, cl_ref, o_ref, high, low):
@@ -67,7 +76,7 @@
 def early_projection(r_all, c_high, c_low):
     _, rows, _ = r_all.shape
     count, width = c_high.shape
-    tile = 128
+    tile = 256 if width % 256 == 0 else 128
     col = pl.BlockSpec((count, tile), lambda j: (0, j))
     return pl.pallas_call(
         early_kernel,
@@ -86,7 +95,7 @@
     sources = [[[refs.pop(0) for _ in range(parts)] for _ in range(2)] for _ in range(pairs)]
     high_ref, low_ref = refs.pop(0), refs.pop(0)
     if last:
-        first_y, second_y, s_ref, scale_ref, acc_ref = (refs.pop(0) for _ in range(5))
+        first_y, second_y, sh_ref, sl_ref, scale_ref, acc_ref = (refs.pop(0) for _ in range(6))
     refs = refs[1:] if last == 2 else refs
     out_ref, staged, q_high, q_low, sems = refs[:5]
     depth = staged.shape[3]
@@ -123,22 +132,27 @@
                 for copy in copies(i + 1):
                     copy.start()
 
-    product = dot3(q_high[...], q_low[...], high_ref[...], low_ref[...])
-
     def emit(mixed):
-        if not last:
+        if last:
+            out_ref[0] = (acc_ref[...] + mixed) * scale_ref[...]
+        else:
             out_ref[...] = mixed
-            return
+
+    if last:
         size = first_y.shape[3]
-        y_high, y_low = refs[5:7]
-
-        @pl.when(col == 0)
+
+        @pl.when(jnp.logical_and(step == 0, col == 0))
         def _():
-            y_high[:, :size], y_low[:, :size] = split2(first_y[0, 0])
-            y_high[:, size:], y_low[:, size:] = split2(second_y[0, 0])
-
-        update = dot3(y_high[...], y_low[...], *split2(s_ref[...]))
-        out_ref[0] = (acc_ref[...] + mixed - update) * scale_ref[...]
+            for at, y_ref in ((2 * depth, first_y), (2 * depth + size, second_y)):
+                span = slice(at, at + size)
+                q_high[:, span], q_low[:, span] = split2(y_ref[0, 0])
+
+    high, low = high_ref[...], low_ref[...]
+    if last:
+        keep = jnp.where(step == 0, 1.0, 0.0).astype(jnp.bfloat16) if pairs > 1 else None
+        extra = [ref[...] if keep is None else ref[...] * keep for ref in (sh_ref, sl_ref)]
+        high, low = jnp.concatenate([high, extra[0]]), jnp.concatenate([low, extra[1]])
+    product = dot3(q_high[...], q_low[...], high, low)
 
     if pairs == 1:
         emit(product)
@@ -177,7 +191,8 @@
     operands += [c_high, c_low]
     count = parts * rows
     scratch = [pltpu.VMEM((2, parts, rows, depth), jnp.float32)]
-    scratch += [pltpu.VMEM((count, 2 * depth), jnp.bfloat16)] * 2
+    inner = 2 * depth + (0 if finish is None else 2 * finish[0].shape[3])
+    scratch += [pltpu.VMEM((count, inner), jnp.bfloat16)] * 2
     scratch += [pltpu.SemaphoreType.DMA((2, parts))]
     aliases, last = {}, 0
     if finish is None:
@@ -191,10 +206,11 @@
             pl.BlockSpec((1, 1, count, size), lambda i, j, info: (0, half, block, 0)),
             pl.BlockSpec((1, 1, count, size), lambda i, j, info: (1, half, block, 0)),
             pl.BlockSpec((2 * size, tile), lambda i, j, info: (0, j)),
+            pl.BlockSpec((2 * size, tile), lambda i, j, info: (0, j)),
             pl.BlockSpec((1, tile), lambda i, j, info: (0, j)),
             pl.BlockSpec((count, tile), lambda i, j, info: (block, j)),
         ]
-        operands += [reflectors, reflectors, s, scale, held]
+        operands += [reflectors, reflectors, *s, scale, held]
         if out is not None:
             in_specs.append(pl.BlockSpec(memory_space=pl.ANY))
             operands.append(out)
@@ -203,7 +219,6 @@
         out_spec = pl.BlockSpec(
             (1, count, tile), lambda i, j, info: (half, block, jnp.where(i == pairs - 1, j, 0))
         )
-        scratch += [pltpu.VMEM((count, 2 * size), jnp.bfloat16)] * 2
     if pairs > 1:
         scratch.append(pltpu.VMEM((width // tile, count, tile), jnp.float32))
     return pl.pallas_call(
@@ -320,7 +335,9 @@
     upper = jnp.triu(triangles)
     s1 = jnp.dot(upper[1], p_all[size:], **exact)
     s0 = jnp.dot(upper[0], p_all[:size] - jnp.dot(cross, s1, **exact), **exact)
-    s = jnp.concatenate([s0, s1], axis=0)
+    s = -jnp.concatenate([s0, s1], axis=0)
+    s_high = lax.reduce_precision(s, 8, 7)
+    s = (s_high.astype(jnp.bfloat16), (s - s_high).astype(jnp.bfloat16))
 
     out = None
     for h in range(2):

time: 613 us -> 567 us (0.925)
  Pallas kernels: 273 us -> 234 us
  local copies, waits for them, and re-layouts: 21.5 us -> 15.3 us
    pallas_call x5, Pallas kernels: 191 us -> 169 us  [rows_call(): pl.pallas_call(functools.partial(rows_kernel, (pairs, parts, rows), last)...]
    pallas_call x1, Pallas kernels: 40.5 us -> 30.4 us  [make_cauchy(): pl.pallas_call(cauchy_kernel, grid=(count // rows,), in_specs=[vec, vec,...]
    pallas_call x1, Pallas kernels: 29.4 us -> 22.2 us  [early_projection(): pl.pallas_call(early_kernel, grid=(width // tile,), in_specs=[pl.BlockSpe...]
    broadcast_in_dim x2 -> x0, local copies, waits for them, and re-layouts: 6.19 us -> none  [the longest x1 3.14 us: make_cauchy(): poles[:, None]]
  transfers between devices with their start and end apart: 33 -> 33, of which waited for: 12 -> 12; matrix products, arithmetic and copies ran while one was open for 6% -> 6% of each run, Pallas kernels for 40% -> 37%
where the time goes in v1:
time: 567 us; the launch traced here: 560 us
  Pallas kernels  234 us (41%)
  waiting for transfers between devices  233 us (41%)
  starting transfers between devices  39.5 us (7%)
  between operations  15.4 us (3%)
  local copies, waits for them, and re-layouts  15.3 us (3%)
  matrix products  12.3 us (2%)
  other arithmetic  10.2 us (2%)
    ppermute x25, waiting for transfers between devices, swap(): return lax.ppermute(x, 'col', [(i, i ^ mask) for i in range(col_count)])  189 us
    pallas_call x5, Pallas kernels, rows_call(): pl.pallas_call(functools.partial(rows_kernel, (pairs, parts, rows), last)...  169 us
    ppermute x6, waiting for transfers between devices, row_swap(): return lax.ppermute(x, 'row', [(i, i ^ mask) for i in range(row_count)])  44 us
    pallas_call x1, Pallas kernels, make_cauchy(): pl.pallas_call(cauchy_kernel, grid=(count // rows,), in_specs=[vec, vec,...  30.4 us
    ppermute x6, starting transfers between devices, row_swap(): return lax.ppermute(x, 'row', [(i, i ^ mask) for i in range(row_count)])  22.8 us
    pallas_call x1, Pallas kernels, early_projection(): pl.pallas_call(early_kernel, grid=(width // tile,), in_specs=[pl.BlockSpe...  22.2 us
    ppermute x25, starting transfers between devices, swap(): return lax.ppermute(x, 'col', [(i, i ^ mask) for i in range(col_count)])  16.7 us
    pallas_call x1, Pallas kernels, project(): pl.pallas_call(project_kernel, grid=(2, 2), in_specs=[pl.BlockSpec((1, 1,...  12.1 us
  transfers between devices with their start and end apart: 33, of which 12 were waited for; matrix products, arithmetic and copies ran while one was open for 6% of the time, Pallas kernels for 37%

profile of v1, /device:TPU:0, one launch (start us, length us, event | category | flops | bytes accessed | tf_op | source)
XLA Modules:
  0.0 559.6 jit_solution(12957323361247503384)
XLA Ops:
  7.4 12.1 %project.1 = f32[2,512,640]{2,1,0:T(8,128)} custom-call(f32[2,2,1280,256]{3,2,1,0:T(8,128)} %refs_5_.3, f32[2,1280,640]{2,1,0:T(8,128)} %refs_1_.3), custom_call_target="tpu_custom_call" | custom-call | tf_op jit(solution)/shard_map/project/pallas_call | solution.py:249
  19.5 1.6 constant_dynamic-slice_fusion.2
  21.1 3.1 collective-permute-start.3
  24.2 2.6 collective-permute-start.4
  26.8 25.4 %collective-permute-done.3 = f32[2,128,640]{2,1,0:T(8,128)S(1)} collective-permute-done((f32[2,128,640]{2,1,0:T(8,128)S(1)}, f32[2,128,640]{2,1,0:T(8,128)S(1)}, u32[]{:S(2)}, u32[]{:S(2)}) %collective-permute-start.3) | collective-permute-done | bytes 655392 | tf_op jit(solution)/shard_map/ppermute | solution.py:277
  52.3 18.6 %collective-permute-done.4 = f32[2,128,640]{2,1,0:T(8,128)S(1)} collective-permute-done((f32[2,128,640]{2,1,0:T(8,128)S(1)}, f32[2,128,640]{2,1,0:T(8,128)S(1)}, u32[]{:S(2)}, u32[]{:S(2)}) %collective-permute-start.4) | collective-permute-done | bytes 655392 | tf_op jit(solution)/shard_map/ppermute | solution.py:277
  70.8 2.3 add_add_fusion
  73.2 3.4 slice_bitcast_fusion
  76.5 1.6 collective-permute-start.21
  78.1 1.5 collective-permute-start.19
  79.6 0.5 collective-permute-start.25
  80.2 0.5 collective-permute-start.28
  80.7 1.5 collective-permute-start
  82.2 45.0 %collective-permute-done.21.refs_5_ = f32[640,640]{1,0:T(8,128)S(1)} collective-permute-done((f32[640,640]{1,0:T(8,128)S(1)}, f32[640,640]{1,0:T(8,128)S(1)}, u32[]{:S(2)}, u32[]{:S(2)}) %collective-permute-start.21) | collective-permute-done | bytes 1638432 | tf_op jit(solution)/shard_map/ppermute | solution.py:274
  127.2 1.4 collective-permute-start.13
  128.6 1.6 collective-permute-done.19.refs_8_
  130.2 41.2 %collective-permute-done.25.refs_4_ = f32[640,640]{1,0:T(8,128)S(1)} collective-permute-done((f32[640,640]{1,0:T(8,128)S(1)}, f32[640,640]{1,0:T(8,128)S(1)}, u32[]{:S(2)}, u32[]{:S(2)}) %collective-permute-start.25) | collective-permute-done | bytes 1638432 | tf_op jit(solution)/shard_map/ppermute | solution.py:274
  171.5 1.5 collective-permute-start.10
  173.0 1.5 collective-permute-start.14
  174.5 32.1 %collective-permute-done.refs_5_ = f32[640,640]{1,0:T(8,128)S(1)} collective-permute-done((f32[640,640]{1,0:T(8,128)S(1)}, f32[640,640]{1,0:T(8,128)S(1)}, u32[]{:S(2)}, u32[]{:S(2)}) %collective-permute-start) | collective-permute-done | bytes 1638432 | tf_op jit(solution)/shard_map/ppermute | solution.py:274
  206.6 1.6 collective-permute-done.13.refs_8_
  208.2 30.2 %collective-permute-done.10.refs_4_ = f32[640,640]{1,0:T(8,128)} collective-permute-done((f32[640,640]{1,0:T(8,128)S(1)}, f32[640,640]{1,0:T(8,128)}, u32[]{:S(2)}, u32[]{:S(2)}) %collective-permute-start.10) | collective-permute-done | bytes 1638432 | tf_op jit(solution)/shard_map/ppermute | solution.py:274
  238.4 1.2 collective-permute-done.14.refs_9_
  239.6 0.8 collective-permute-start.20
  240.4 1.5 collective-permute-start.22
  241.9 0.1 collective-permute-start.12
  242.0 2.2 collective-permute-done.30.refs_11_
  244.2 0.1 collective-permute-start.15
  244.3 33.6 %collective-permute-done.20.refs_0_ = f32[640,640]{1,0:T(8,128)} collective-permute-done((f32[640,640]{1,0:T(8,128)S(1)}, f32[640,640]{1,0:T(8,128)}, u32[]{:S(2)}, u32[]{:S(2)}) %collective-permute-start.20) | collective-permute-done | bytes 1638432 | tf_op jit(solution)/shard_map/ppermute | solution.py:274
  277.9 0.2 collective-permute-done.22.refs_1_
  278.2 0.3 collective-permute-start.16
  278.5 7.5 %fusion.10 = f32[256,256]{1,0:T(8,128)} fusion(f32[2,2,1280,256]{3,2,1,0:T(8,128)} %refs_5_.3), kind=kOutput, calls=%fused_computation.20 | convolution fusion | flops 2013265920 | bytes 5505024 | tf_op jit(solution)/shard_map/hrb,hrd->bd/dot_general | solution.py:306
  286.1 0.6 compare_select_fusion
  286.7 1.3 collective-permute-start.17
  287.9 1.5 collective-permute-start.1
  289.5 0.8 compare_select_fusion.1
  290.2 7.5 %gather_fusion = f32[1280]{0:T(1024)S(1)} fusion(f32[10240]{0:T(1024)S(1)} %get-tuple-element.27, s32[2048]{0:T(1024)S(1)} %pad_clamp_fusion), kind=kCustom, calls=%fused_computation | custom fusion | bytes 15360 | tf_op jit(solution)/shard_map/jit(_take)/gather | solution.py:310
  297.8 0.8 dynamic-slice_select_fusion
  298.6 0.6 broadcast_in_dim.45.key_ref
  299.2 0.6 select_n.62.root_ref
  299.8 30.4 %cauchy.1 = (bf16[10240,1280]{1,0:T(8,128)(2,1)}, bf16[10240,1280]{1,0:T(8,128)(2,1)}, f32[1,1280]{1,0:T(1,128)}) custom-call(f32[1,10240]{1,0:T(1,128)} %bitcast.54, f32[1,10240]{1,0:T(1,128)} %bitcast.53, f32[1,1280]{1,0:T(1,128)} %select_n.62.root_ref, s32[1,1280]{1,0:T(1,128)} %broadcast_in_dim.45.key_ref), custom_call_target="tpu_custom_call" | custom-call | tf_op jit(solution)/shard_map/cauchy/pallas_call | solution.py:55
  330.2 0.7 stack.80.info_ref
  330.9 0.6 stack.73.info_ref
  331.4 0.7 pad_add_fusion.info_ref
  332.1 0.7 add_add_fusion.1
  332.8 0.1 iota_compare_fusion
  332.9 22.2 %early.1 = f32[128,1280]{1,0:T(8,128)} custom-call(f32[2,128,5120]{2,1,0:T(8,128)} %all-gather.2.cloned.1.call-done.r_ref, bf16[10240,1280]{1,0:T(8,128)(2,1)} %get-tuple-element.8.ch_ref.refs_12_.refs_4_.refs_2_, bf16[10240,1280]{1,0:T(8,128)(2,1)} %get-tuple-element.9.cl_ref.refs_13_.refs_5_.refs_3_), custom_call_target="tpu_custom_call" | custom-call | tf_op jit(solution)/shard_map/early/pallas_call | solution.py:81
  355.1 14.5 %collective-permute-start.6 = (f32[128,1280]{1,0:T(8,128)}, f32[128,1280]{1,0:T(8,128)}, u32[]{:S(2)}, u32[]{:S(2)}) collective-permute-start(f32[128,1280]{1,0:T(8,128)} %early.1), channel_id=1, source_target_pairs={{0,8},{8,0},{16,24},{24,16},{1,9},{9,1},{17,25},{25,17},{2,10},{10... | collective-permute-start | bytes 1966088 | tf_op jit(solution)/shard_map/ppermute | solution.py:277
  369.6 1.1 collective-permute-start.7
  370.7 1.5 collective-permute-start.8
  372.2 0.6 reshape_select_fusion.refs_10_.refs_8_
  372.9 53.6 %shard_map.83.refs_11_ = f32[1280,1280]{1,0:T(8,128)} custom-call(s32[6]{0:T(128)} %stack.80.info_ref, f32[2,1280,640]{2,1,0:T(8,128)} %refs_1_.3, f32[2,1280,640]{2,1,0:T(8,128)} %refs_1_.3, f32[2,1280,640]{2,1,0:T(8,128)} %collective-permute-done.9.refs_2_.refs_3_, f32[2,1280,640]{2,1,0:T(8,128)} %collective-permute-done.9.refs_2_.refs_3_, ...), custom_call_target="tpu_custom_call" | custom-call | tf_op jit(solution)/shard_map/pallas_call | solution.py:224
  426.4 53.9 %shard_map.82.refs_9_ = f32[1280,1280]{1,0:T(8,128)} custom-call(s32[6]{0:T(128)} %stack.73.info_ref, f32[2,1280,640]{2,1,0:T(8,128)} %refs_1_.3, f32[2,1280,640]{2,1,0:T(8,128)} %refs_1_.3, f32[2,1280,640]{2,1,0:T(8,128)} %collective-permute-done.9.refs_2_.refs_3_, f32[2,1280,640]{2,1,0:T(8,128)} %collective-permute-done.9.refs_2_.refs_3_, ...), custom_call_target="tpu_custom_call" | custom-call | tf_op jit(solution)/shard_map/pallas_call | solution.py:224
  480.4 0.5 collective-permute-start.24
  481.0 0.4 collective-permute-start.2
  481.4 1.7 pad_maximum_fusion
  483.2 0.3 dynamic-slice_bitcast_fusion.3
  483.4 1.2 fusion.6
  484.7 2.2 convolution_subtract_fusion
  486.9 1.3 fusion.15
  488.2 1.9 fusion
  490.1 28.4 %shard_map.84.refs_10_ = f32[2,1280,1280]{2,1,0:T(8,128)} custom-call(s32[4]{0:T(128)} %pad_add_fusion.info_ref, f32[640,640]{1,0:T(8,128)} %collective-permute-done.20.refs_0_, f32[640,640]{1,0:T(8,128)} %collective-permute-done.22.refs_1_, f32[640,640]{1,0:T(8,128)} %collective-permute-done.23.refs_2_, f32[640,640]{1,0:T(8,128)} %collective-permute-done.24.refs_3_, ...), custom_call_target="tpu_custom_call" | custom-call | tf_op jit(solution)/shard_map/pallas_call | solution.py:224
  518.5 16.7 %shard_map.85.refs_10_ = f32[2,1280,1280]{2,1,0:T(8,128)} custom-call(s32[4]{0:T(128)} %get-tuple-element.30.info_ref, f32[640,640]{1,0:T(8,128)} %collective-permute-done.17.refs_0_, f32[640,640]{1,0:T(8,128)} %collective-permute-done.18.refs_1_, ...), custom_call_target="tpu_custom_call", output_to_operand_aliasing={{}: (11, {})} | custom-call | tf_op jit(solution)/shard_map/pallas_call | solution.py:224
  535.2 16.7 %shard_map.86 = f32[2,1280,1280]{2,1,0:T(8,128)} custom-call(s32[4]{0:T(128)} %get-tuple-element.29.info_ref, f32[640,640]{1,0:T(8,128)} %collective-permute-done.1.refs_0_, f32[640,640]{1,0:T(8,128)} %collective-permute-done.2.refs_1_, bf16[10240,1280]{1,0:T(8,128)(2,1)} %get-tuple-element.8.ch_ref.refs_12_.refs_4_.refs_2_, ...), custom_call_target="tpu_custom_call", output_to_operand_aliasing={{}: (11, {})} | custom-call | tf_op jit(solution)/shard_map/pallas_call | solution.py:224
  (69 shorter events, 0.5 us)
Async XLA Ops:
  7.4 325.5 %all-gather.2.cloned.1.call-start = ((), (), s32[]{:S(2)}) async-start(), calls=%async_computation | async-start | bytes 5898240 | tf_op jit(solution)/shard_map/all_gather | solution.py:305
  21.1 31.1 %collective-permute-start.3 = (f32[2,128,640]{2,1,0:T(8,128)S(1)}, f32[2,128,640]{2,1,0:T(8,128)S(1)}, u32[]{:S(2)}, u32[]{:S(2)}) collective-permute-start(f32[2,128,640]{2,1,0:T(8,128)S(1)} %get-tuple-element.24), channel_id=1, source_target_pairs={{0,8},{8,0},{16,24},{24,16},{1,9},{9,1},{17,25},{25,17},{2,10},{10... | collective-permute-start | bytes 1966088 | tf_op jit(solution)/shard_map/ppermute | solution.py:277
  24.2 46.6 %collective-permute-start.4 = (f32[2,128,640]{2,1,0:T(8,128)S(1)}, f32[2,128,640]{2,1,0:T(8,128)S(1)}, u32[]{:S(2)}, u32[]{:S(2)}) collective-permute-start(f32[2,128,640]{2,1,0:T(8,128)S(1)} %get-tuple-element.26), channel_id=1, source_target_pairs={{0,16},{8,24},{16,0},{24,8},{1,17},{9,25},{17,1},{25,9},{2,18},{10... | collective-permute-start | bytes 1966088 | tf_op jit(solution)/shard_map/ppermute | solution.py:277
  26.8 44.0 %collective-permute-start.5 = (f32[2,128,640]{2,1,0:T(8,128)S(1)}, f32[2,128,640]{2,1,0:T(8,128)}, u32[]{:S(2)}, u32[]{:S(2)}) collective-permute-start(f32[2,128,640]{2,1,0:T(8,128)S(1)} %get-tuple-element.25), channel_id=1, source_target_pairs={{0,24},{8,16},{16,8},{24,0},{1,25},{9,17},{17,9},{25,1},{2,26},{10... | collective-permute-start | bytes 1966088 | tf_op jit(solution)/shard_map/ppermute | solution.py:277
  73.1 411.6 %all-reduce.2.cloned.1.call-start = ((), (), s32[]{:S(2)}) async-start(), calls=%async_computation.1 | async-start | bytes 524288 | tf_op jit(solution)/shard_map/psum | solution.py:306
  76.5 50.6 %collective-permute-start.21 = (f32[640,640]{1,0:T(8,128)S(1)}, f32[640,640]{1,0:T(8,128)S(1)}, u32[]{:S(2)}, u32[]{:S(2)}) collective-permute-start(f32[640,640]{1,0:T(8,128)S(1)} %get-tuple-element.14), channel_id=1, source_target_pairs={{0,2},{1,3},{2,0},{3,1},{4,6},{5,7},{6,4},{7,5},{8,10},{9,11},{10,... | collective-permute-start | bytes 4915208 | tf_op jit(solution)/shard_map/ppermute | solution.py:274
  78.1 52.1 %collective-permute-start.19 = (f32[640,640]{1,0:T(8,128)S(1)}, f32[640,640]{1,0:T(8,128)S(1)}, u32[]{:S(2)}, u32[]{:S(2)}) collective-permute-start(f32[640,640]{1,0:T(8,128)S(1)} %get-tuple-element.15), channel_id=1, source_target_pairs={{0,4},{1,5},{2,6},{3,7},{4,0},{5,1},{6,2},{7,3},{8,12},{9,13},{10,... | collective-permute-start | bytes 4915208 | tf_op jit(solution)/shard_map/ppermute | solution.py:274
  79.6 91.8 %collective-permute-start.25 = (f32[640,640]{1,0:T(8,128)S(1)}, f32[640,640]{1,0:T(8,128)S(1)}, u32[]{:S(2)}, u32[]{:S(2)}) collective-permute-start(f32[640,640]{1,0:T(8,128)S(1)} %get-tuple-element.15), channel_id=1, source_target_pairs={{0,2},{1,3},{2,0},{3,1},{4,6},{5,7},{6,4},{7,5},{8,10},{9,11},{10,... | collective-permute-start | bytes 4915208 | tf_op jit(solution)/shard_map/ppermute | solution.py:274
  80.2 92.8 %collective-permute-start.28 = (f32[640,640]{1,0:T(8,128)S(1)}, f32[640,640]{1,0:T(8,128)S(1)}, u32[]{:S(2)}, u32[]{:S(2)}) collective-permute-start(f32[640,640]{1,0:T(8,128)S(1)} %get-tuple-element.14), channel_id=1, source_target_pairs={{0,4},{1,5},{2,6},{3,7},{4,0},{5,1},{6,2},{7,3},{8,12},{9,13},{10,... | collective-permute-start | bytes 4915208 | tf_op jit(solution)/shard_map/ppermute | solution.py:274
  80.7 125.9 %collective-permute-start = (f32[640,640]{1,0:T(8,128)S(1)}, f32[640,640]{1,0:T(8,128)S(1)}, u32[]{:S(2)}, u32[]{:S(2)}) collective-permute-start(f32[640,640]{1,0:T(8,128)S(1)} %get-tuple-element.17), channel_id=1, source_target_pairs={{0,2},{1,3},{2,0},{3,1},{4,6},{5,7},{6,4},{7,5},{8,10},{9,11},{10,... | collective-permute-start | bytes 4915208 | tf_op jit(solution)/shard_map/ppermute | solution.py:274
  127.2 114.7 %copy-start.2 = (f32[640,640]{1,0:T(8,128)}, f32[640,640]{1,0:T(8,128)S(1)}, u32[]{:S(2)}) copy-start(f32[640,640]{1,0:T(8,128)S(1)} %collective-permute-done.21.refs_5_) | copy-start | bytes 4915204
  127.2 158.8 %copy-start.11 = (f32[10240]{0:T(1024)S(1)}, f32[10240]{0:T(1024)}, u32[]{:S(2)}) copy-start(f32[10240]{0:T(1024)} %param.11) | copy-start | bytes 122884
  127.2 158.9 %copy-start.12 = (s32[10240]{0:T(1024)S(1)}, s32[10240]{0:T(1024)}, u32[]{:S(2)}) copy-start(s32[10240]{0:T(1024)} %param.13) | copy-start | bytes 122884
  127.2 158.9 %copy-start.13 = (f32[10240]{0:T(1024)S(1)}, f32[10240]{0:T(1024)}, u32[]{:S(2)}) copy-start(f32[10240]{0:T(1024)} %param.10) | copy-start | bytes 122884
  127.2 81.0 %collective-permute-start.13 = (f32[640,640]{1,0:T(8,128)S(1)}, f32[640,640]{1,0:T(8,128)}, u32[]{:S(2)}, u32[]{:S(2)}) collective-permute-start(f32[640,640]{1,0:T(8,128)S(1)} %get-tuple-element.16), channel_id=1, source_target_pairs={{0,4},{1,5},{2,6},{3,7},{4,0},{5,1},{6,2},{7,3},{8,12},{9,13},{10,... | collective-permute-start | bytes 4915208 | tf_op jit(solution)/shard_map/ppermute | solution.py:274
  130.2 147.9 %copy-start.3 = (f32[640,640]{1,0:T(8,128)}, f32[640,640]{1,0:T(8,128)S(1)}, u32[]{:S(2)}) copy-start(f32[640,640]{1,0:T(8,128)S(1)} %collective-permute-done.19.refs_8_) | copy-start | bytes 4915204
  130.2 240.5 %collective-permute-start.9 = (f32[2,1280,640]{2,1,0:T(8,128)}, f32[2,1280,640]{2,1,0:T(8,128)}, u32[]{:S(2)}, u32[]{:S(2)}) collective-permute-start(f32[2,1280,640]{2,1,0:T(8,128)} %refs_1_.3), channel_id=1, source_target_pairs={{0,1},{1,0},{2,3},{3,2},{4,5},{5,4},{6,7},{7,6},{8,9},{9,8},{10,11... | collective-permute-start | bytes 19660808 | tf_op jit(solution)/shard_map/ppermute | solution.py:274
  171.5 107.0 %copy-start.4 = (f32[640,640]{1,0:T(8,128)}, f32[640,640]{1,0:T(8,128)S(1)}, u32[]{:S(2)}) copy-start(f32[640,640]{1,0:T(8,128)S(1)} %collective-permute-done.25.refs_4_) | copy-start | bytes 4915204
  171.5 66.9 %collective-permute-start.10 = (f32[640,640]{1,0:T(8,128)S(1)}, f32[640,640]{1,0:T(8,128)}, u32[]{:S(2)}, u32[]{:S(2)}) collective-permute-start(f32[640,640]{1,0:T(8,128)S(1)} %get-tuple-element.16), channel_id=1, source_target_pairs={{0,2},{1,3},{2,0},{3,1},{4,6},{5,7},{6,4},{7,5},{8,10},{9,11},{10,... | collective-permute-start | bytes 4915208 | tf_op jit(solution)/shard_map/ppermute | solution.py:274
  173.0 105.5 %copy-start.5 = (f32[640,640]{1,0:T(8,128)}, f32[640,640]{1,0:T(8,128)S(1)}, u32[]{:S(2)}) copy-start(f32[640,640]{1,0:T(8,128)S(1)} %collective-permute-done.28.refs_9_) | copy-start | bytes 4915204
  173.0 66.6 %collective-permute-start.14 = (f32[640,640]{1,0:T(8,128)S(1)}, f32[640,640]{1,0:T(8,128)}, u32[]{:S(2)}, u32[]{:S(2)}) collective-permute-start(f32[640,640]{1,0:T(8,128)S(1)} %get-tuple-element.17), channel_id=1, source_target_pairs={{0,4},{1,5},{2,6},{3,7},{4,0},{5,1},{6,2},{7,3},{8,12},{9,13},{10,... | collective-permute-start | bytes 4915208 | tf_op jit(solution)/shard_map/ppermute | solution.py:274
  206.6 81.4 %copy-start.1 = (f32[640,640]{1,0:T(8,128)}, f32[640,640]{1,0:T(8,128)S(1)}, u32[]{:S(2)}) copy-start(f32[640,640]{1,0:T(8,128)S(1)} %collective-permute-done.refs_5_) | copy-start | bytes 4915204
  206.6 33.0 %collective-permute-start.27 = (f32[640,640]{1,0:T(8,128)S(1)}, f32[640,640]{1,0:T(8,128)S(1)}, u32[]{:S(2)}, u32[]{:S(2)}) collective-permute-start(f32[640,640]{1,0:T(8,128)S(1)} %collective-permute-done.21.refs_5_), channel_id=1, source_target_pairs={{0,1},{1,0},{2,3},{3,2},{4,5},{5,4},{6,7},{7,6},{8,9},{9,8},{10,11... | collective-permute-start | bytes 4915208 | tf_op jit(solution)/shard_map/ppermute | solution.py:274
  208.2 32.2 %collective-permute-start.29 = (f32[640,640]{1,0:T(8,128)S(1)}, f32[640,640]{1,0:T(8,128)S(1)}, u32[]{:S(2)}, u32[]{:S(2)}) collective-permute-start(f32[640,640]{1,0:T(8,128)S(1)} %collective-permute-done.19.refs_8_), channel_id=1, source_target_pairs={{0,1},{1,0},{2,3},{3,2},{4,5},{5,4},{6,7},{7,6},{8,9},{9,8},{10,11... | collective-permute-start | bytes 4915208 | tf_op jit(solution)/shard_map/ppermute | solution.py:274
  238.4 3.5 collective-permute-start.26
  239.6 4.6 collective-permute-start.30
  239.6 38.8 %copy-start.6 = (f32[640,640]{1,0:T(8,128)}, f32[640,640]{1,0:T(8,128)S(1)}, u32[]{:S(2)}) copy-start(f32[640,640]{1,0:T(8,128)S(1)} %collective-permute-done.27.refs_7_) | copy-start | bytes 4915204
  239.6 38.3 %collective-permute-start.20 = (f32[640,640]{1,0:T(8,128)S(1)}, f32[640,640]{1,0:T(8,128)}, u32[]{:S(2)}, u32[]{:S(2)}) collective-permute-start(f32[640,640]{1,0:T(8,128)S(1)} %collective-permute-done.19.refs_8_), channel_id=1, source_target_pairs={{0,2},{1,3},{2,0},{3,1},{4,6},{5,7},{6,4},{7,5},{8,10},{9,11},{10,... | collective-permute-start | bytes 4915208 | tf_op jit(solution)/shard_map/ppermute | solution.py:274
  240.4 38.1 %copy-start.7 = (f32[640,640]{1,0:T(8,128)}, f32[640,640]{1,0:T(8,128)S(1)}, u32[]{:S(2)}) copy-start(f32[640,640]{1,0:T(8,128)S(1)} %collective-permute-done.29.refs_10_) | copy-start | bytes 4915204
  240.4 37.8 %collective-permute-start.22 = (f32[640,640]{1,0:T(8,128)S(1)}, f32[640,640]{1,0:T(8,128)}, u32[]{:S(2)}, u32[]{:S(2)}) collective-permute-start(f32[640,640]{1,0:T(8,128)S(1)} %collective-permute-done.21.refs_5_), channel_id=1, source_target_pairs={{0,4},{1,5},{2,6},{3,7},{4,0},{5,1},{6,2},{7,3},{8,12},{9,13},{10,... | collective-permute-start | bytes 4915208 | tf_op jit(solution)/shard_map/ppermute | solution.py:274
  241.9 36.5 %copy-start.8 = (f32[640,640]{1,0:T(8,128)}, f32[640,640]{1,0:T(8,128)S(1)}, u32[]{:S(2)}) copy-start(f32[640,640]{1,0:T(8,128)S(1)} %collective-permute-done.26.refs_6_) | copy-start | bytes 4915204
  241.9 44.8 %collective-permute-start.12 = (f32[640,640]{1,0:T(8,128)S(1)}, f32[640,640]{1,0:T(8,128)}, u32[]{:S(2)}, u32[]{:S(2)}) collective-permute-start(f32[640,640]{1,0:T(8,128)S(1)} %collective-permute-done.refs_5_), channel_id=1, source_target_pairs={{0,1},{1,0},{2,3},{3,2},{4,5},{5,4},{6,7},{7,6},{8,9},{9,8},{10,11... | collective-permute-start | bytes 4915208 | tf_op jit(solution)/shard_map/ppermute | solution.py:274
  244.2 34.2 %copy-start.9 = (f32[640,640]{1,0:T(8,128)}, f32[640,640]{1,0:T(8,128)S(1)}, u32[]{:S(2)}) copy-start(f32[640,640]{1,0:T(8,128)S(1)} %collective-permute-done.30.refs_11_) | copy-start | bytes 4915204
  244.2 43.7 %collective-permute-start.15 = (f32[640,640]{1,0:T(8,128)}, f32[640,640]{1,0:T(8,128)}, u32[]{:S(2)}, u32[]{:S(2)}) collective-permute-start(f32[640,640]{1,0:T(8,128)} %collective-permute-done.13.refs_8_), channel_id=1, source_target_pairs={{0,1},{1,0},{2,3},{3,2},{4,5},{5,4},{6,7},{7,6},{8,9},{9,8},{10,11... | collective-permute-start | bytes 4915208 | tf_op jit(solution)/shard_map/ppermute | solution.py:274
  277.9 77.2 %collective-permute-start.11 = (f32[640,640]{1,0:T(8,128)}, f32[640,640]{1,0:T(8,128)}, u32[]{:S(2)}, u32[]{:S(2)}) collective-permute-start(f32[640,640]{1,0:T(8,128)} %collective-permute-done.10.refs_4_), channel_id=1, source_target_pairs={{0,1},{1,0},{2,3},{3,2},{4,5},{5,4},{6,7},{7,6},{8,9},{9,8},{10,11... | collective-permute-start | bytes 4915208 | tf_op jit(solution)/shard_map/ppermute | solution.py:274
  278.2 91.5 %collective-permute-start.16 = (f32[640,640]{1,0:T(8,128)}, f32[640,640]{1,0:T(8,128)}, u32[]{:S(2)}, u32[]{:S(2)}) collective-permute-start(f32[640,640]{1,0:T(8,128)} %collective-permute-done.14.refs_9_), channel_id=1, source_target_pairs={{0,1},{1,0},{2,3},{3,2},{4,5},{5,4},{6,7},{7,6},{8,9},{9,8},{10,11... | collective-permute-start | bytes 4915208 | tf_op jit(solution)/shard_map/ppermute | solution.py:274
  286.7 193.6 %collective-permute-start.17 = (f32[640,640]{1,0:T(8,128)}, f32[640,640]{1,0:T(8,128)}, u32[]{:S(2)}, u32[]{:S(2)}) collective-permute-start(f32[640,640]{1,0:T(8,128)} %collective-permute-done.13.refs_8_), channel_id=1, source_target_pairs={{0,2},{1,3},{2,0},{3,1},{4,6},{5,7},{6,4},{7,5},{8,10},{9,11},{10,... | collective-permute-start | bytes 4915208 | tf_op jit(solution)/shard_map/ppermute | solution.py:274
  287.9 192.5 %collective-permute-start.1 = (f32[640,640]{1,0:T(8,128)S(1)}, f32[640,640]{1,0:T(8,128)}, u32[]{:S(2)}, u32[]{:S(2)}) collective-permute-start(f32[640,640]{1,0:T(8,128)S(1)} %collective-permute-done.refs_5_), channel_id=1, source_target_pairs={{0,4},{1,5},{2,6},{3,7},{4,0},{5,1},{6,2},{7,3},{8,12},{9,13},{10,... | collective-permute-start | bytes 4915208 | tf_op jit(solution)/shard_map/ppermute | solution.py:274
  332.9 39.3 %copy-start.10 = (f32[2,256,256]{2,1,0:T(8,128)S(1)}, f32[2,256,256]{2,1,0:T(8,128)}, u32[]{:S(2)}) copy-start(f32[2,256,256]{2,1,0:T(8,128)} %param.15) | copy-start | bytes 1572868
  332.9 39.3 %copy-start.14 = (f32[1,1280]{1,0:T(1,128)S(1)}, f32[1,1280]{1,0:T(1,128)}, u32[]{:S(2)}) copy-start(f32[1,1280]{1,0:T(1,128)} %get-tuple-element.10) | copy-start | bytes 15364
  355.1 125.8 %collective-permute-start.6 = (f32[128,1280]{1,0:T(8,128)}, f32[128,1280]{1,0:T(8,128)}, u32[]{:S(2)}, u32[]{:S(2)}) collective-permute-start(f32[128,1280]{1,0:T(8,128)} %early.1), channel_id=1, source_target_pairs={{0,8},{8,0},{16,24},{24,16},{1,9},{9,1},{17,25},{25,17},{2,10},{10... | collective-permute-start | bytes 1966088 | tf_op jit(solution)/shard_map/ppermute | solution.py:277
  369.6 111.4 %collective-permute-start.7 = (f32[128,1280]{1,0:T(8,128)}, f32[128,1280]{1,0:T(8,128)}, u32[]{:S(2)}, u32[]{:S(2)}) collective-permute-start(f32[128,1280]{1,0:T(8,128)} %early.1), channel_id=1, source_target_pairs={{0,16},{8,24},{16,0},{24,8},{1,17},{9,25},{17,1},{25,9},{2,18},{10... | collective-permute-start | bytes 1966088 | tf_op jit(solution)/shard_map/ppermute | solution.py:277
  370.7 110.7 %collective-permute-start.8 = (f32[128,1280]{1,0:T(8,128)}, f32[128,1280]{1,0:T(8,128)}, u32[]{:S(2)}, u32[]{:S(2)}) collective-permute-start(f32[128,1280]{1,0:T(8,128)} %early.1), channel_id=1, source_target_pairs={{0,24},{8,16},{16,8},{24,0},{1,25},{9,17},{17,9},{25,1},{2,26},{10... | collective-permute-start | bytes 1966088 | tf_op jit(solution)/shard_map/ppermute | solution.py:277
  426.4 55.0 %copy-start = (f32[128,1280]{1,0:T(8,128)S(1)}, f32[128,1280]{1,0:T(8,128)}, u32[]{:S(2)}) copy-start(f32[128,1280]{1,0:T(8,128)} %early.1) | copy-start | bytes 1966084
  480.3 9.8 %collective-permute-start.23 = (f32[640,640]{1,0:T(8,128)}, f32[640,640]{1,0:T(8,128)}, u32[]{:S(2)}, u32[]{:S(2)}) collective-permute-start(f32[640,640]{1,0:T(8,128)} %collective-permute-done.20.refs_0_), channel_id=1, source_target_pairs={{0,1},{1,0},{2,3},{3,2},{4,5},{5,4},{6,7},{7,6},{8,9},{9,8},{10,11... | collective-permute-start | bytes 4915208 | tf_op jit(solution)/shard_map/ppermute | solution.py:274
  480.4 9.7 %collective-permute-start.24 = (f32[640,640]{1,0:T(8,128)}, f32[640,640]{1,0:T(8,128)}, u32[]{:S(2)}, u32[]{:S(2)}) collective-permute-start(f32[640,640]{1,0:T(8,128)} %collective-permute-done.22.refs_1_), channel_id=1, source_target_pairs={{0,1},{1,0},{2,3},{3,2},{4,5},{5,4},{6,7},{7,6},{8,9},{9,8},{10,11... | collective-permute-start | bytes 4915208 | tf_op jit(solution)/shard_map/ppermute | solution.py:274
  480.9 37.6 %collective-permute-start.18 = (f32[640,640]{1,0:T(8,128)}, f32[640,640]{1,0:T(8,128)}, u32[]{:S(2)}, u32[]{:S(2)}) collective-permute-start(f32[640,640]{1,0:T(8,128)} %collective-permute-done.17.refs_0_), channel_id=1, source_target_pairs={{0,1},{1,0},{2,3},{3,2},{4,5},{5,4},{6,7},{7,6},{8,9},{9,8},{10,11... | collective-permute-start | bytes 4915208 | tf_op jit(solution)/shard_map/ppermute | solution.py:274
  481.0 54.2 %collective-permute-start.2 = (f32[640,640]{1,0:T(8,128)}, f32[640,640]{1,0:T(8,128)}, u32[]{:S(2)}, u32[]{:S(2)}) collective-permute-start(f32[640,640]{1,0:T(8,128)} %collective-permute-done.1.refs_0_), channel_id=1, source_target_pairs={{0,1},{1,0},{2,3},{3,2},{4,5},{5,4},{6,7},{7,6},{8,9},{9,8},{10,11... | collective-permute-start | bytes 4915208 | tf_op jit(solution)/shard_map/ppermute | solution.py:274
Sparse Core Ops, SparseCore 0:
  73.2 74.1 all-gather.1
Sparse Core Ops, SparseCore 1:
  286.1 48.6 all-reduce.1
